TPU v7x, 256 devices: a whole 4x4x8 slice. The times are simulated.
256 devices in a mesh: shell: 8 (over z), sector: 32 (over x, y, core).
Axes of the slice: x: 4, y: 4, z: 8, core: 2. Of those that a mesh axis runs over, the one named last changes fastest.
Arguments:
- bricks: bfloat16 [8, 256, 32, 512], P('shell', 'sector'), may hold values from -6 to 6
- conv_w: bfloat16 [32, 864], replicated, may hold values from -0.21875 to 0.21875
- conv_b: float32 [32], replicated, may hold values from -3 to 3
- head_w1: bfloat16 [32, 64], replicated, may hold values from -1 to 1
- head_b1: float32 [64], replicated, may hold values from -3 to 3
- head_w2: float32 [64, 2], replicated, may hold values from -0.75 to 0.75
- queries: int32 [8, 1024, 256], P('shell', 'sector'), may hold values from -1 to 4095, as said below
- sample_src: int32 [8, 131072], P('shell', 'sector'), may hold values from 0 to 8191, as said below
- depth_target: float32 [16384], P('sector'), may hold values from 0.1 to 0.9
- inten_target: float32 [16384], P('sector'), may hold values from 0 to 1
- drop_label: int32 [16384], P('sector'), may hold values 0 or 1
Outputs:
- loss_mean: float32 [], replicated
- grad_conv_w: float32 [32, 864], replicated
- grad_conv_b: float32 [32], replicated
- grad_head_w1: float32 [32, 64], replicated
- grad_head_b1: float32 [64], replicated
- grad_head_w2: float32 [64, 2], replicated
- grad_bricks: bfloat16 [8, 256, 32, 512], P('shell', 'sector')
- ray_depth: float32 [16384], P('sector')
Inputs may be any that keep to these rules, and one draw needn't show every extreme that they name: `queries`: entry of the buffer from a device of sector v to owner w: a cell address (brick of the owner times 512 plus cell) or -1 for an empty slot. Every sample of a device holds exactly one live slot, named by sample_src as w * 256 + slot. In every shell one owner receives full buffers of 256 from every sector. `sample_src`: A slot w * 256 + slot of the sample's own device; distinct samples of a device have distinct slots.
All inputs are finite; a program needn't handle non-finite values. No bound on the sum of `drop_label` on one device may be relied on, other than what follows from the above.
Results may differ from a plain program's by a relative error of at most 0.0015.
The roundings to bfloat16 on the way count: a program that leaves them out, or rounds other values in their place, can miss the bound.
Values may be sent and summed in bfloat16 or wider, within the bound.
No kernel may reach another device: no remote copies, remote signals or barrier semaphores. Data moves between devices by JAX's collectives and lax.ppermute only.
A program may use at most 192 MiB of HBM per device.

v0:
```python
import math
import jax
import jax.numpy as jnp
from jax import lax
from jax.sharding import PartitionSpec as P

SAMP = 8
HIGHEST = lax.Precision.HIGHEST
CUBE_OFFSETS = [(a, b, c) for a in range(3) for b in range(3) for c in range(3)]


def entering(value, axis, join, neutral, backward):
    count, mine = (lax.axis_size(axis), lax.axis_index(axis))
    pieces = lax.all_gather(value, axis)
    if backward:
        pieces = pieces[::-1]
        mine = count - 1 - mine
    total = jnp.full_like(value, 0) + jnp.asarray(neutral, value.dtype)

    def hop(position, total):
        longer = join(total, pieces[position])
        return jnp.where(position < mine, longer, total)

    return lax.fori_loop(0, count - 1, hop, total)


def unfold_cells(block_set):
    brick_count = block_set.shape[0]
    channel_width = block_set.shape[1]
    cube = block_set.reshape(brick_count, channel_width, 8, 8, 8)
    padded = jnp.pad(cube, ((0, 0), (0, 0), (1, 1), (1, 1), (1, 1)))
    columns = [
        padded[:, :, a : a + 8, b : b + 8, c : c + 8].reshape(brick_count, channel_width, 512)
        for a, b, c in CUBE_OFFSETS
    ]
    return jnp.stack(columns, axis=1).reshape(brick_count, 27 * channel_width, 512)


def conv_backward(block_set, block_cot, conv_w, conv_b):
    unfolded = unfold_cells(block_set)
    pre_act = (
        jnp.einsum("oc,bcn->obn", conv_w, unfolded, preferred_element_type=jnp.float32)
        + conv_b[:, None, None]
    )
    _, gelu_pull = jax.vjp(jax.nn.gelu, pre_act)
    pre_grad = gelu_pull(block_cot)[0].astype(jnp.bfloat16)
    weight_grad = jnp.einsum("obn,bcn->oc", pre_grad, unfolded, preferred_element_type=jnp.float32)
    bias_grad = jnp.sum(pre_grad.astype(jnp.float32), axis=(1, 2))
    column_grad = jnp.einsum("oc,obn->bcn", conv_w, pre_grad, preferred_element_type=jnp.float32)
    _, fold_pull = jax.vjp(unfold_cells, jnp.zeros(block_set.shape, jnp.float32))
    block_grad = fold_pull(column_grad)[0]
    return (weight_grad, bias_grad, block_grad.astype(jnp.bfloat16))


def field_head(feature_cols, weight_one, bias_one, weight_two):
    hidden = (
        jnp.einsum("ch,cm->hm", weight_one, feature_cols, precision=HIGHEST) + bias_one[:, None]
    )
    outputs = jnp.einsum("hk,hm->km", weight_two, jax.nn.gelu(hidden), precision=HIGHEST)
    return (jax.nn.softplus(outputs[0]), jax.nn.sigmoid(outputs[1]))


def render_terms(density, intensity, depth_grid, step_size):
    optical = density * step_size
    before = jnp.cumsum(optical, axis=-1) - optical
    weights = jnp.exp(-before) * (1.0 - jnp.exp(-optical))
    return (
        jnp.sum(weights * depth_grid, axis=-1),
        jnp.sum(weights * intensity, axis=-1),
        jnp.sum(optical, axis=-1),
    )


def add_terms(first_term, second_term):
    return first_term + second_term


def local(
    bricks,
    conv_w,
    conv_b,
    head_w1,
    head_b1,
    head_w2,
    queries,
    sample_src,
    depth_target,
    inten_target,
    drop_label,
):
    shells = lax.axis_size("shell")
    sectors = lax.axis_size("sector")
    shell_index = lax.axis_index("shell")
    local_bricks = bricks[0]
    brick_count = local_bricks.shape[0]
    channels = local_bricks.shape[1]
    group_size = math.gcd(brick_count, 8)
    group_cols = group_size * 512
    group_total = brick_count // group_size
    weight_one = head_w1.astype(jnp.float32)
    brick_groups = local_bricks.reshape(group_total, group_size, channels, 512)

    def decode_group(group_id, table_now):
        block_set = lax.dynamic_index_in_dim(brick_groups, group_id, 0, keepdims=False)
        pre_act = (
            jnp.einsum(
                "oc,bcn->obn", conv_w, unfold_cells(block_set), preferred_element_type=jnp.float32
            )
            + conv_b[:, None, None]
        )
        values = jax.nn.gelu(pre_act).astype(jnp.bfloat16).reshape(channels, group_cols)
        return values

    cell_table = lax.fori_loop(
        0, group_total, decode_group, jnp.zeros((channels, brick_count * 512), jnp.bfloat16)
    )
    requests = queries[0]
    capacity = requests.shape[1]
    owner_addr = lax.all_to_all(
        requests, "sector", split_axis=0, concat_axis=0, tiled=True
    ).reshape(-1)
    live_slot = owner_addr >= 0
    picked = jnp.take(cell_table, jnp.where(live_slot, owner_addr, 0), axis=1)
    owner_feats = jnp.where(live_slot[None, :], picked, jnp.zeros((), jnp.bfloat16))
    sources = sample_src[0]
    replies = lax.all_to_all(
        owner_feats.reshape(channels, sectors, capacity),
        "sector",
        split_axis=1,
        concat_axis=1,
        tiled=True,
    )
    sample_cols = jnp.take(replies.reshape(channels, sectors * capacity), sources, axis=1).astype(
        jnp.float32
    )
    (density, intensity), head_pull = jax.vjp(field_head, sample_cols, weight_one, head_b1, head_w2)
    ray_count = sources.shape[0] // SAMP
    density = density.reshape(ray_count, SAMP)
    intensity = intensity.reshape(ray_count, SAMP)
    step_size = 2.0 / (shells * SAMP)
    depth_grid = (
        shell_index.astype(jnp.float32) * SAMP + jnp.arange(SAMP, dtype=jnp.float32) + 0.5
    ) / (shells * SAMP)

    def local_render(dens_in, inten_in):
        return render_terms(dens_in, inten_in, depth_grid, step_size)

    (shell_depth, shell_inten, shell_tau), render_pull = jax.vjp(local_render, density, intensity)
    dropped = drop_label.astype(jnp.float32)
    kept_weight = 1.0 - dropped
    zeros_rays = jnp.zeros_like(shell_tau)
    prefix = entering(shell_tau, "shell", add_terms, zeros_rays, False)
    entry_trans = jnp.exp(-prefix)
    ray_depth, ray_inten, tau_total = lax.psum(
        (entry_trans * shell_depth, entry_trans * shell_inten, shell_tau), "shell"
    )
    escape = jnp.exp(-tau_total)
    grad_depth = 2.0 * kept_weight * (ray_depth - depth_target)
    grad_inten = 2.0 * kept_weight * (ray_inten - inten_target)
    own_weight = (grad_depth * shell_depth + grad_inten * shell_inten) * entry_trans
    behind = entering(own_weight, "shell", add_terms, zeros_rays, True)
    grad_escape = 2.0 * (escape - dropped)
    dens_grad, inten_grad = render_pull(
        (grad_depth * entry_trans, grad_inten * entry_trans, -grad_escape * escape - behind)
    )
    ray_loss = jnp.sum(
        kept_weight * ((ray_depth - depth_target) ** 2 + (ray_inten - inten_target) ** 2)
        + (escape - dropped) ** 2
    )
    loss_mean = lax.psum(ray_loss, "sector") / (ray_count * sectors)
    sample_grad, grad_one, grad_bias_one, grad_two = head_pull(
        (dens_grad.reshape(-1), inten_grad.reshape(-1))
    )
    buckets = jnp.zeros((channels, sectors * capacity), jnp.float32).at[:, sources].set(sample_grad)
    owner_grad = lax.all_to_all(
        buckets.reshape(channels, sectors, capacity),
        "sector",
        split_axis=1,
        concat_axis=1,
        tiled=True,
    ).reshape(channels, sectors * capacity)
    target_index = jnp.where(live_slot, owner_addr, brick_count * 512)
    table_grad = (
        jnp.zeros((channels, brick_count * 512), jnp.float32)
        .at[:, target_index]
        .add(owner_grad, mode="drop")
    )

    def conv_back(totals, group_id):
        block_set = lax.dynamic_index_in_dim(brick_groups, group_id, 0, keepdims=False)
        block_cot = table_grad.reshape(channels, group_size, 512)
        weight_grad, bias_grad, block_grad = conv_backward(block_set, block_cot, conv_w, conv_b)
        return ((totals[0] + weight_grad, totals[1] + bias_grad), block_grad)

    start = (jnp.zeros(conv_w.shape, jnp.float32), jnp.zeros_like(conv_b))
    (conv_grad, conv_bias_grad), brick_grads = lax.scan(
        conv_back, start, jnp.arange(group_total, dtype=jnp.int32)
    )
    summed = lax.psum(
        (conv_grad, conv_bias_grad, grad_one, grad_bias_one, grad_two), ("shell", "sector")
    )
    return (
        loss_mean,
        summed[0],
        summed[1],
        summed[2],
        summed[3],
        summed[4],
        brick_grads,
        ray_depth,
    )


def solution(mesh):
    return jax.shard_map(
        local,
        mesh=mesh,
        in_specs=(
            P("shell", "sector", None, None),
            P(),
            P(),
            P(),
            P(),
            P(),
            P("shell", "sector", None),
            P("shell", "sector"),
            P("sector"),
            P("sector"),
            P("sector"),
        ),
        out_specs=(P(), P(), P(), P(), P(), P(), P("shell", "sector", None, None), P("sector")),
        check_vma=False,
    )
```

profile of v0, /device:TPU:1, one launch (start us, length us, event | category | flops | bytes accessed | tf_op | source)
XLA Modules:
  0.0 665.0 jit_solution(13087959850178110753)
XLA Ops:
  8.6 8.6 %all-to-all-start = ((s32[32,1,256]{2,1,0:T(1,128)}), s32[32,1,256]{2,1,0:T(1,128)S(1)}, u32[]{:S(2)}, u32[]{:S(2)}) async-start(s32[32,1,256]{2,1,0:T(1,128)} %all_to_all.12), calls=%async_computation | async-start | bytes 65536 | tf_op jit(solution)/shard_map/all_to_all | solution.py:119
  18.6 3.4 pad_slice_fusion.1
  22.1 6.8 %pad_slice_fusion = (bf16[8,32,8,8,8]{1,4,3,2,0:T(8,128)(2,1)}, bf16[8,32,8,8,8]{1,4,3,2,0:T(8,128)(2,1)}, bf16[8,32,8,8,8]{1,4,3,2,0:T(8,128)(2,1)}, bf16[8,32,...) fusion(bf16[8,32,8,8,8]{1,4,3,2,0:T(8,128)(2,1)S(1)} %bitcast.139), kind=kLoop, calls=%fused_computation.8 | loop fusion | bytes 5242880 | tf_op jit(solution)/shard_map/while/body/eval_jaxpr/slice | solution.py:33
  118.1 5.1 multiply_convert_fusion
  124.4 24.0 %gather_fusion = bf16[8192,32]{1,0:T(8,128)(2,1)S(1)} fusion(bf16[32,4096]{0,1:T(8,128)(2,1)S(1)} %bitcast.136, s32[8192]{0:T(1024)S(1)} %broadcast_clamp_fusion), kind=kCustom, calls=%fused_computation | custom fusion | bytes 1081344 | tf_op jit(solution)/shard_map/jit(_take)/gather | solution.py:123
  150.3 7.4 %all-to-all-start.1 = ((bf16[32,32,256]{2,0,1:T(8,128)(2,1)}), bf16[32,32,256]{2,0,1:T(8,128)(2,1)S(1)}, u32[]{:S(2)}, u32[]{:S(2)}) async-start(bf16[32,32,256]{2,0,1:T(8,128)(2,1)} %select_select_fusion), calls=%async_computation.1 | async-start | bytes 1048576 | tf_op jit(solution)/shard_map/all_to_all | solution.py:126
  157.8 11.5 %all-to-all-done.1 = bf16[32,32,256]{2,0,1:T(8,128)(2,1)S(1)} async-done(((bf16[32,32,256]{2,0,1:T(8,128)(2,1)}), bf16[32,32,256]{2,0,1:T(8,128)(2,1)S(1)}, u32[]{:S(2)}, u32[]{:S(2)}) %all-to-all-start.1) | async-done | bytes 524320 | tf_op jit(solution)/shard_map/all_to_all | solution.py:126
  170.4 12.1 %gather_fusion.1 = bf16[4096,32]{1,0:T(8,128)(2,1)S(1)} fusion(bf16[32,8192]{0,1:T(8,128)(2,1)S(1)} %bitcast.163, s32[4096]{0:T(1024)S(1)} %broadcast_clamp_fusion.1), kind=kCustom, calls=%fused_computation.1 | custom fusion | bytes 540672 | tf_op jit(solution)/shard_map/jit(_take)/gather | solution.py:133
  187.0 19.6 %all-gather.2 = f32[8,1,512]{2,1,0:T(1,128)S(1)} all-gather(f32[1,1,512]{2,1,0:T(1,128)S(1)} %bitcast.209), channel_id=2, replica_groups=mesh['shell'=8,'sector'=32] {'shell'}, dimensions={0}, use_global_device_ids=true | all-gather | bytes 18432 | tf_op jit(solution)/shard_map/all_gather | solution.py:14
  207.0 11.4 %all-reduce.31 = (f32[512]{0:T(512)S(1)}, f32[512]{0:T(512)S(1)}, f32[512]{0:T(512)S(1)}) all-reduce(f32[512]{0:T(512)S(1)} %get-tuple-element.265, f32[512]{0:T(512)S(1)} %get-tuple-element.360, f32[512]{0:T(512)S(1)} %get-tuple-element.359), channel_id=1, replica_groups=mesh['shell'=8,'sector'=32] {'shell'}, use_global_device_ids=true, to_apply=%region_8.9 | all-reduce | flops 1536 | bytes 12288 | tf_op jit(solution)/shard_map/psum | solution.py:154
  220.8 15.9 %all-gather.3 = f32[8,1,512]{2,1,0:T(1,128)S(1)} all-gather(f32[1,1,512]{2,1,0:T(1,128)} %bitcast.210), channel_id=3, replica_groups=mesh['shell'=8,'sector'=32] {'shell'}, dimensions={0}, use_global_device_ids=true | all-gather | bytes 18432 | tf_op jit(solution)/shard_map/all_gather | solution.py:14
  239.9 2.4 fusion.56
  242.3 3.9 fusion.57
  246.2 13.2 %scatter_custom_fusion = f32[32,8192]{0,1:T(8,128)} fusion(s32[4096]{0:T(1024)S(1)} %bitcast.205, f32[4096,32]{1,0:T(8,128)} %fusion.57, f32[]{:T(128)} %constant.164.clone.1), kind=kCustom, calls=%fused_computation.45 | custom fusion | bytes 1049088 | tf_op jit(solution)/shard_map/scatter | solution.py:174
  259.5 3.6 copy.154
  263.1 18.7 %all-to-all-start.2 = ((f32[32,32,256]{2,0,1:T(8,128)}), f32[32,32,256]{2,0,1:T(8,128)S(1)}, u32[]{:S(2)}, u32[]{:S(2)}) async-start(f32[32,32,256]{2,0,1:T(8,128)} %copy.154), calls=%async_computation.2 | async-start | bytes 2097152 | tf_op jit(solution)/shard_map/all_to_all | solution.py:175
  281.8 71.8 %psum.66 = f32[]{:T(128)} all-reduce(f32[]{:T(128)} %get-tuple-element.354), channel_id=1, replica_groups=mesh['shell'=8,'sector'=32] {'sector'}, use_global_device_ids=true, to_apply=%region_10.11 | all-reduce | flops 1 | bytes 8 | tf_op jit(solution)/shard_map/psum | solution.py:170
  358.3 2.8 copy.156
  361.1 45.0 %scatter_custom_fusion.1 = f32[32,4096]{0,1:T(8,128)S(1)} fusion(s32[8192]{0:T(1024)} %bitcast.208, f32[8192,32]{1,0:T(8,128)} %copy.156, f32[]{:T(128)} %constant.164.clone.1), kind=kCustom, calls=%fused_computation.58 | custom fusion | flops 262144 | bytes 524800 | tf_op jit(solution)/shard_map/scatter-add | solution.py:186
  407.2 5.8 convolution_bitcast_fusion.2
  417.1 3.4 fusion.54
  422.1 3.0 copy.197
  425.1 3.0 copy.204
  428.1 3.0 copy.203
  431.0 3.0 copy.202
  434.0 3.0 copy.201
  437.0 3.0 copy.200
  440.0 3.0 copy.199
  443.0 3.0 copy.223
  445.9 3.0 copy.222
  448.9 3.0 copy.221
  451.9 3.0 copy.220
  454.9 3.0 copy.219
  457.9 3.0 copy.218
  460.9 3.0 copy.217
  463.9 3.0 copy.216
  466.9 3.0 copy.215
  469.8 3.0 copy.214
  472.8 3.0 copy.213
  475.9 3.0 copy.212
  478.8 3.0 copy.211
  481.8 3.0 copy.210
  484.8 3.0 copy.209
  487.8 3.0 copy.208
  490.8 3.2 copy.207
  497.9 16.8 %pad_add_fusion = f32[8,32,10,10,10]{1,4,3,2,0:T(8,128)S(1)} fusion(f32[8,32,8,8,8]{1,4,3,2,0:T(8,128)} %bitcast.148, f32[8,32,8,8,8]{1,4,3,2,0:T(8,128)} %bitcast.149, f32[8,32,8,8,8]{1,4,3,2,0:T(8,128)} %bitcast.150, f32[8,32,8,8,8]{1,4,3,2,0:T(8,128)} %bitcast.151, f32[8,32,8,8,8]{1,4,3,2,0:T(8,128)} %bitcast.152, f32[8,32,8,8,8]{1,4,3,2,0:T(8,128)} %bitcast.153, ...), kind=kLoop, calls=%fused_computation.34 | loop fusion | flops 5376000 | bytes 12558336 | tf_op jit(solution)/shard_map/while/body/eval_jaxpr/transpose(jvp())/add_any | solution.py:33
  515.8 72.8 %all-reduce.30 = (f32[32]{0:T(128)}, f32[32,64]{1,0:T(8,128)}, f32[64]{0:T(128)}, f32[64,2]{0,1:T(2,128)}) all-reduce(f32[32]{0:T(128)S(1)} %get-tuple-element.289, f32[32,64]{1,0:T(8,128)S(1)} %fusion.21, f32[64]{0:T(128)S(1)} %get-tuple-element.363, f32[64,2]{0,1:T(2,128)S(1)} %fusion.20), channel_id=1, replica_groups=mesh['shell'=8,'sector'=32] {'shell','sector'}, use_global_device_ids=true, to_apply=%region_18.19 | all-reduce | flops 2272 | bytes 18176 | tf_op jit(solution)/shard_map/psum | solution.py:199
  589.7 65.3 %all-reduce.34.cloned.1.call-done = f32[32,864]{1,0:T(8,128)} async-done(((f32[32,864]{1,0:T(8,128)}), f32[32,864]{1,0:T(8,128)}) %all-reduce.34.cloned.1.call-update) | async-done | bytes 110608 | tf_op jit(solution)/shard_map/psum | solution.py:199
  (200 shorter events, 125.2 us)
Async XLA Ops:
  7.2 110.9 %copy-start = (bf16[32,864]{1,0:T(8,128)(2,1)S(1)}, bf16[32,864]{1,0:T(8,128)(2,1)}, u32[]{:S(2)}) copy-start(bf16[32,864]{1,0:T(8,128)(2,1)} %param.16) | copy-start | bytes 165892
  8.6 115.1 %all-to-all-start = ((s32[32,1,256]{2,1,0:T(1,128)}), s32[32,1,256]{2,1,0:T(1,128)S(1)}, u32[]{:S(2)}, u32[]{:S(2)}) async-start(s32[32,1,256]{2,1,0:T(1,128)} %all_to_all.12), calls=%async_computation | async-start | bytes 65536 | tf_op jit(solution)/shard_map/all_to_all | solution.py:119
  22.1 6.8 %copy-start.18 = (s32[1,4096]{1,0:T(1,128)S(1)}, s32[1,4096]{1,0:T(1,128)}, u32[]{:S(2)}) copy-start(s32[1,4096]{1,0:T(1,128)} %param.22) | copy-start | bytes 49156
  28.9 13.6 %copy-start.9 = (bf16[8,32,8,8,8]{1,4,3,2,0:T(8,128)(2,1)S(1)}, bf16[8,32,8,8,8]{1,4,3,2,0:T(8,128)(2,1)}, u32[]{:S(2)}) copy-start(bf16[8,32,8,8,8]{1,4,3,2,0:T(8,128)(2,1)} %get-tuple-element.345) | copy-start | bytes 786436
  43.6 22.6 %copy-start.8 = (bf16[8,32,8,8,8]{1,4,3,2,0:T(8,128)(2,1)S(1)}, bf16[8,32,8,8,8]{1,4,3,2,0:T(8,128)(2,1)}, u32[]{:S(2)}) copy-start(bf16[8,32,8,8,8]{1,4,3,2,0:T(8,128)(2,1)} %get-tuple-element.330) | copy-start | bytes 786436
  61.7 30.3 %copy-start.12 = (bf16[1,8,32,512]{3,2,1,0:T(8,128)(2,1)S(1)}, bf16[1,8,32,512]{3,2,1,0:T(8,128)(2,1)}, u32[]{:S(2)}) copy-start(bf16[1,8,32,512]{3,2,1,0:T(8,128)(2,1)} %param.15) | copy-start | bytes 786436
  67.2 32.2 %copy-start.7 = (bf16[8,32,8,8,8]{1,4,3,2,0:T(8,128)(2,1)S(1)}, bf16[8,32,8,8,8]{1,4,3,2,0:T(8,128)(2,1)}, u32[]{:S(2)}) copy-start(bf16[8,32,8,8,8]{1,4,3,2,0:T(8,128)(2,1)} %get-tuple-element.336) | copy-start | bytes 786436
  92.7 23.9 %copy-start.13 = (bf16[8,1,32,512]{3,2,1,0:T(8,128)(2,1)S(1)}, bf16[8,1,32,512]{3,2,1,0:T(8,128)(2,1)}, u32[]{:S(2)}) copy-start(bf16[8,1,32,512]{3,2,1,0:T(8,128)(2,1)} %copy.147) | copy-start | bytes 786436
  95.0 23.1 %copy-start.27 = (f32[32]{0:T(128)S(1)}, f32[32]{0:T(128)}, u32[]{:S(2)}) copy-start(f32[32]{0:T(128)} %param.17) | copy-start | bytes 388
  100.5 13.9 %copy-start.17 = (bf16[8,1,32,512]{3,2,1,0:T(8,128)(2,1)S(1)}, bf16[8,1,32,512]{3,2,1,0:T(8,128)(2,1)}, u32[]{:S(2)}) copy-start(bf16[8,1,32,512]{3,2,1,0:T(8,128)(2,1)} %copy.144) | copy-start | bytes 786436
  100.5 14.6 %copy-start.15 = (bf16[8,1,32,512]{3,2,1,0:T(8,128)(2,1)S(1)}, bf16[8,1,32,512]{3,2,1,0:T(8,128)(2,1)}, u32[]{:S(2)}) copy-start(bf16[8,1,32,512]{3,2,1,0:T(8,128)(2,1)} %copy.145) | copy-start | bytes 786436
  100.5 15.3 %copy-start.14 = (bf16[8,1,32,512]{3,2,1,0:T(8,128)(2,1)S(1)}, bf16[8,1,32,512]{3,2,1,0:T(8,128)(2,1)}, u32[]{:S(2)}) copy-start(bf16[8,1,32,512]{3,2,1,0:T(8,128)(2,1)} %copy.146) | copy-start | bytes 786436
  100.5 16.8 %copy-start.16 = (bf16[8,1,32,512]{3,2,1,0:T(8,128)(2,1)S(1)}, bf16[8,1,32,512]{3,2,1,0:T(8,128)(2,1)}, u32[]{:S(2)}) copy-start(bf16[8,1,32,512]{3,2,1,0:T(8,128)(2,1)} %copy.148) | copy-start | bytes 786436
  124.4 58.2 %copy-start.19 = (bf16[32,64]{1,0:T(8,128)(2,1)S(1)}, bf16[32,64]{1,0:T(8,128)(2,1)}, u32[]{:S(2)}) copy-start(bf16[32,64]{1,0:T(8,128)(2,1)} %param.18) | copy-start | bytes 12292
  124.4 58.2 %copy-start.28 = (f32[64]{0:T(128)S(1)}, f32[64]{0:T(128)}, u32[]{:S(2)}) copy-start(f32[64]{0:T(128)} %param.19) | copy-start | bytes 772
  148.4 35.0 %copy-start.29 = (f32[64,2]{0,1:T(2,128)S(1)}, f32[64,2]{0,1:T(2,128)}, u32[]{:S(2)}) copy-start(f32[64,2]{0,1:T(2,128)} %param.20) | copy-start | bytes 1540
  150.3 19.0 %all-to-all-start.1 = ((bf16[32,32,256]{2,0,1:T(8,128)(2,1)}), bf16[32,32,256]{2,0,1:T(8,128)(2,1)S(1)}, u32[]{:S(2)}, u32[]{:S(2)}) async-start(bf16[32,32,256]{2,0,1:T(8,128)(2,1)} %select_select_fusion), calls=%async_computation.1 | async-start | bytes 1048576 | tf_op jit(solution)/shard_map/all_to_all | solution.py:126
  157.7 48.9 %copy-start.26 = (f32[8]{0:T(128)}, f32[8]{0:T(128)S(1)}, u32[]{:S(2)}) copy-start(f32[8]{0:T(128)S(1)} %add_multiply_fusion.1) | copy-start | bytes 100
  157.8 60.7 %copy-start.21 = (s32[512]{0:T(512)S(1)}, s32[512]{0:T(512)}, u32[]{:S(2)}) copy-start(s32[512]{0:T(512)} %param.25) | copy-start | bytes 6148
  157.8 60.7 %copy-start.23 = (f32[512]{0:T(512)S(1)}, f32[512]{0:T(512)}, u32[]{:S(2)}) copy-start(f32[512]{0:T(512)} %param.24) | copy-start | bytes 6148
  157.8 60.7 %copy-start.24 = (f32[512]{0:T(512)S(1)}, f32[512]{0:T(512)}, u32[]{:S(2)}) copy-start(f32[512]{0:T(512)} %param.23) | copy-start | bytes 6148
  183.4 58.9 %copy-start.11 = (f32[64,4096]{1,0:T(8,128)}, f32[64,4096]{1,0:T(8,128)S(1)}, u32[]{:S(2)}) copy-start(f32[64,4096]{1,0:T(8,128)S(1)} %fusion) | copy-start | bytes 3145732
  218.4 1.2 copy-start.22
  218.5 1.2 copy-start.25
  219.7 0.9 copy-start.20
  263.1 95.2 %all-to-all-start.2 = ((f32[32,32,256]{2,0,1:T(8,128)}), f32[32,32,256]{2,0,1:T(8,128)S(1)}, u32[]{:S(2)}, u32[]{:S(2)}) async-start(f32[32,32,256]{2,0,1:T(8,128)} %copy.154), calls=%async_computation.2 | async-start | bytes 2097152 | tf_op jit(solution)/shard_map/all_to_all | solution.py:175
  281.7 373.3 %all-reduce.34.cloned.1.call-start = ((), (), s32[]{:S(2)}) async-start(), calls=%async_computation.3 | async-start | bytes 229376 | tf_op jit(solution)/shard_map/psum | solution.py:199
  358.2 48.5 %copy-start.10 = (f32[32,8,512]{2,0,1:T(8,128)S(1)}, f32[32,8,512]{2,0,1:T(8,128)}, u32[]{:S(2)}) copy-start(f32[32,8,512]{2,0,1:T(8,128)} %get-tuple-element.362) | copy-start | bytes 1572868
  497.9 16.8 %copy-start.2 = (f32[8,1,32,512]{2,3,0,1:T(8,128)S(1)}, f32[8,1,32,512]{2,3,0,1:T(8,128)}, u32[]{:S(2)}) copy-start(f32[8,1,32,512]{2,3,0,1:T(8,128)} %copy.223) | copy-start | bytes 1572868
  497.9 16.8 %copy-start.3 = (f32[8,1,32,512]{2,3,0,1:T(8,128)S(1)}, f32[8,1,32,512]{2,3,0,1:T(8,128)}, u32[]{:S(2)}) copy-start(f32[8,1,32,512]{2,3,0,1:T(8,128)} %copy.222) | copy-start | bytes 1572868
  497.9 16.8 %copy-start.4 = (f32[8,1,32,512]{2,3,0,1:T(8,128)S(1)}, f32[8,1,32,512]{2,3,0,1:T(8,128)}, u32[]{:S(2)}) copy-start(f32[8,1,32,512]{2,3,0,1:T(8,128)} %copy.221) | copy-start | bytes 1572868
  497.9 16.8 %copy-start.5 = (f32[8,1,32,512]{2,3,0,1:T(8,128)S(1)}, f32[8,1,32,512]{2,3,0,1:T(8,128)}, u32[]{:S(2)}) copy-start(f32[8,1,32,512]{2,3,0,1:T(8,128)} %copy.220) | copy-start | bytes 1572868
  497.9 16.8 %copy-start.6 = (f32[8,1,32,512]{2,3,0,1:T(8,128)S(1)}, f32[8,1,32,512]{2,3,0,1:T(8,128)}, u32[]{:S(2)}) copy-start(f32[8,1,32,512]{2,3,0,1:T(8,128)} %copy.219) | copy-start | bytes 1572868
  514.7 141.9 %copy-start.1 = (bf16[32,864]{1,0:T(8,128)(2,1)S(1)}, bf16[32,864]{1,0:T(8,128)(2,1)}, u32[]{:S(2)}) copy-start(bf16[32,864]{1,0:T(8,128)(2,1)} %param.16) | copy-start | bytes 165892
Sparse Core Ops, SparseCore 0:
  420.6 234.3 all-reduce.33
where the time goes:
time: 677 us; the launch traced here: 665 us
  local copies, waits for them, and re-layouts  249 us (37%)
  blocking collectives  192 us (28%)
  waiting for transfers between devices  76.9 us (11%)
  other arithmetic  70.1 us (10%)
  starting transfers between devices  34.7 us (5%)
  matrix products  25.1 us (4%)
  between operations  16.9 us (2%)
    unnamed x118, local copies, waits for them, and re-layouts  119 us
    psum x1, blocking collectives, local(): lax.psum((conv_grad, conv_bias_grad, grad_one, grad_bias_one, grad_two),...  72.8 us
    psum x1, blocking collectives, local(): loss_mean = lax.psum(ray_loss, 'sector') / (ray_count * sectors)  71.8 us
    psum x1, waiting for transfers between devices, local(): lax.psum((conv_grad, conv_bias_grad, grad_one, grad_bias_one, grad_two),...  65.3 us
    reshape x26, local copies, waits for them, and re-layouts, unfold_cells(): jnp.stack(columns, axis=1).reshape(brick_count, 27 * channel_width, 512)  51.4 us
    scatter-add x1, other arithmetic, local(): table_grad = jnp.zeros((channels, brick_count * 512), jnp.float32).at[:,...  45 us
    all_gather x2, blocking collectives, entering(): pieces = lax.all_gather(value, axis)  35.5 us
    gather x2, local copies, waits for them, and re-layouts, local(): picked = jnp.take(cell_table, jnp.where(live_slot, owner_addr, 0), axis=1)  25 us
  transfers between devices with their start and end apart: 4, of which 2 were waited for; matrix products, arithmetic and copies ran while one was open for 31% of the time, Pallas kernels for 0%

commit v1 on v0

--- a/solution.py
+++ b/solution.py
@@ -196,9 +196,9 @@
     (conv_grad, conv_bias_grad), brick_grads = lax.scan(
         conv_back, start, jnp.arange(group_total, dtype=jnp.int32)
     )
-    summed = lax.psum(
-        (conv_grad, conv_bias_grad, grad_one, grad_bias_one, grad_two), ("shell", "sector")
-    )
+    summed = (conv_grad, conv_bias_grad, grad_one, grad_bias_one, grad_two)
+    for mesh_axis in ("sector", "shell"):
+        summed = lax.psum(summed, mesh_axis)
     return (
         loss_mean,
         summed[0],

time: 677 us -> 650 us (0.960)
  the two profiles are of different devices: /device:TPU:1 before, /device:TPU:0 now
where the time goes in v1:
time: 650 us; the launch traced here: 638 us
  local copies, waits for them, and re-layouts  248 us (38%)
  blocking collectives  221 us (34%)
  other arithmetic  75.5 us (12%)
  waiting for transfers between devices  34.1 us (5%)
  matrix products  25.1 us (4%)
  starting transfers between devices  17.6 us (3%)
  between operations  16.8 us (3%)
    psum x1, blocking collectives, local(): loss_mean = lax.psum(ray_loss, 'sector') / (ray_count * sectors)  128 us
    unnamed x108, local copies, waits for them, and re-layouts  117 us
    reshape x26, local copies, waits for them, and re-layouts, unfold_cells(): jnp.stack(columns, axis=1).reshape(brick_count, 27 * channel_width, 512)  51.4 us
    all_gather x2, blocking collectives, entering(): pieces = lax.all_gather(value, axis)  46.4 us
    scatter-add x1, other arithmetic, local(): table_grad = jnp.zeros((channels, brick_count * 512), jnp.float32).at[:,...  44.8 us
    psum x1, blocking collectives, local(): summed = lax.psum(summed, mesh_axis)  30.8 us
    gather x2, local copies, waits for them, and re-layouts, local(): picked = jnp.take(cell_table, jnp.where(live_slot, owner_addr, 0), axis=1)  25 us
    add_any x1, other arithmetic, unfold_cells(): padded[:, :, a:a + 8, b:b + 8, c:c + 8]  18.2 us
  transfers between devices with their start and end apart: 5, of which 3 were waited for; matrix products, arithmetic and copies ran while one was open for 33% of the time, Pallas kernels for 0%

profile of v1, /device:TPU:0, one launch (start us, length us, event | category | flops | bytes accessed | tf_op | source)
XLA Modules:
  0.0 638.1 jit_solution(3421869750454156180)
XLA Ops:
  8.6 5.6 all-to-all-start
  15.6 3.4 pad_slice_fusion.1
  19.0 6.8 %pad_slice_fusion = (bf16[8,32,8,8,8]{1,4,3,2,0:T(8,128)(2,1)}, bf16[8,32,8,8,8]{1,4,3,2,0:T(8,128)(2,1)}, bf16[8,32,8,8,8]{1,4,3,2,0:T(8,128)(2,1)}, bf16[8,32,...) fusion(bf16[8,32,8,8,8]{1,4,3,2,0:T(8,128)(2,1)S(1)} %bitcast.139), kind=kLoop, calls=%fused_computation.8 | loop fusion | bytes 5242880 | tf_op jit(solution)/shard_map/while/body/eval_jaxpr/slice | solution.py:33
  115.1 5.1 multiply_convert_fusion
  121.4 24.0 %gather_fusion = bf16[8192,32]{1,0:T(8,128)(2,1)S(1)} fusion(bf16[32,4096]{0,1:T(8,128)(2,1)S(1)} %bitcast.136, s32[8192]{0:T(1024)S(1)} %broadcast_clamp_fusion), kind=kCustom, calls=%fused_computation | custom fusion | bytes 1081344 | tf_op jit(solution)/shard_map/jit(_take)/gather | solution.py:123
  147.4 7.4 %all-to-all-start.1 = ((bf16[32,32,256]{2,0,1:T(8,128)(2,1)}), bf16[32,32,256]{2,0,1:T(8,128)(2,1)S(1)}, u32[]{:S(2)}, u32[]{:S(2)}) async-start(bf16[32,32,256]{2,0,1:T(8,128)(2,1)} %select_select_fusion), calls=%async_computation.1 | async-start | bytes 1048576 | tf_op jit(solution)/shard_map/all_to_all | solution.py:126
  154.9 11.1 %all-to-all-done.1 = bf16[32,32,256]{2,0,1:T(8,128)(2,1)S(1)} async-done(((bf16[32,32,256]{2,0,1:T(8,128)(2,1)}), bf16[32,32,256]{2,0,1:T(8,128)(2,1)S(1)}, u32[]{:S(2)}, u32[]{:S(2)}) %all-to-all-start.1) | async-done | bytes 524320 | tf_op jit(solution)/shard_map/all_to_all | solution.py:126
  167.0 12.1 %gather_fusion.1 = bf16[4096,32]{1,0:T(8,128)(2,1)S(1)} fusion(bf16[32,8192]{0,1:T(8,128)(2,1)S(1)} %bitcast.163, s32[4096]{0:T(1024)S(1)} %broadcast_clamp_fusion.1), kind=kCustom, calls=%fused_computation.1 | custom fusion | bytes 540672 | tf_op jit(solution)/shard_map/jit(_take)/gather | solution.py:133
  183.6 25.4 %all-gather.2 = f32[8,1,512]{2,1,0:T(1,128)S(1)} all-gather(f32[1,1,512]{2,1,0:T(1,128)S(1)} %bitcast.209), channel_id=2, replica_groups=mesh['shell'=8,'sector'=32] {'shell'}, dimensions={0}, use_global_device_ids=true | all-gather | bytes 18432 | tf_op jit(solution)/shard_map/all_gather | solution.py:14
  209.4 15.7 %all-reduce.32 = (f32[512]{0:T(512)S(1)}, f32[512]{0:T(512)S(1)}, f32[512]{0:T(512)S(1)}) all-reduce(f32[512]{0:T(512)S(1)} %get-tuple-element.265, f32[512]{0:T(512)S(1)} %get-tuple-element.365, f32[512]{0:T(512)S(1)} %get-tuple-element.364), channel_id=1, replica_groups=mesh['shell'=8,'sector'=32] {'shell'}, use_global_device_ids=true, to_apply=%region_8.9 | all-reduce | flops 1536 | bytes 12288 | tf_op jit(solution)/shard_map/psum | solution.py:154
  227.4 21.0 %all-gather.3 = f32[8,1,512]{2,1,0:T(1,128)S(1)} all-gather(f32[1,1,512]{2,1,0:T(1,128)} %bitcast.210), channel_id=3, replica_groups=mesh['shell'=8,'sector'=32] {'shell'}, dimensions={0}, use_global_device_ids=true | all-gather | bytes 18432 | tf_op jit(solution)/shard_map/all_gather | solution.py:14
  254.0 4.0 fusion.57
  257.9 13.2 %scatter_custom_fusion = f32[32,8192]{0,1:T(8,128)} fusion(s32[4096]{0:T(1024)S(1)} %bitcast.205, f32[4096,32]{1,0:T(8,128)} %fusion.57, f32[]{:T(128)} %constant.164.clone.1), kind=kCustom, calls=%fused_computation.45 | custom fusion | bytes 1049088 | tf_op jit(solution)/shard_map/scatter | solution.py:174
  271.1 3.6 copy.154
  274.7 4.3 all-to-all-start.2
  283.0 12.8 %all-to-all-done.2 = f32[32,32,256]{2,0,1:T(8,128)S(1)} async-done(((f32[32,32,256]{2,0,1:T(8,128)}), f32[32,32,256]{2,0,1:T(8,128)S(1)}, u32[]{:S(2)}, u32[]{:S(2)}) %all-to-all-start.2) | async-done | bytes 1048608 | tf_op jit(solution)/shard_map/all_to_all | solution.py:175
  298.7 44.8 %scatter_custom_fusion.1 = f32[32,4096]{0,1:T(8,128)S(1)} fusion(s32[8192]{0:T(1024)} %bitcast.208, f32[8192,32]{1,0:T(8,128)} %copy.156, f32[]{:T(128)} %constant.164.clone.1), kind=kCustom, calls=%fused_computation.58 | custom fusion | flops 262144 | bytes 524800 | tf_op jit(solution)/shard_map/scatter-add | solution.py:186
  344.5 5.8 convolution_bitcast_fusion.2
  354.2 3.6 fusion.54
  359.8 3.0 copy.197
  362.8 3.0 copy.204
  365.8 3.0 copy.203
  368.8 3.0 copy.202
  371.8 3.0 copy.201
  374.8 3.0 copy.200
  377.8 3.0 copy.199
  380.7 3.0 copy.218
  383.7 3.0 copy.217
  386.7 3.0 copy.216
  389.8 3.0 copy.215
  392.8 3.0 copy.214
  395.7 3.0 copy.213
  398.7 2.9 copy.212
  401.6 3.0 copy.211
  404.7 3.0 copy.210
  407.7 3.0 copy.209
  410.7 3.0 copy.208
  413.7 3.0 copy.207
  416.6 3.0 copy.206
  419.6 3.0 copy.205
  422.6 18.2 %pad_add_fusion = f32[8,32,10,10,10]{1,4,3,2,0:T(8,128)} fusion(f32[8,32,8,8,8]{1,4,3,2,0:T(8,128)} %bitcast.148, f32[8,32,8,8,8]{1,4,3,2,0:T(8,128)} %bitcast.149, f32[8,32,8,8,8]{1,4,3,2,0:T(8,128)} %bitcast.150, f32[8,32,8,8,8]{1,4,3,2,0:T(8,128)} %bitcast.151, f32[8,32,8,8,8]{1,4,3,2,0:T(8,128)} %bitcast.152, f32[8,32,8,8,8]{1,4,3,2,0:T(8,128)} %bitcast.153, ...), kind=kLoop, calls=%fused_computation.34 | loop fusion | flops 5376000 | bytes 12558336 | tf_op jit(solution)/shard_map/while/body/eval_jaxpr/transpose(jvp())/add_any | solution.py:33
  441.4 3.0 copy.222
  444.4 3.0 copy.221
  447.5 3.0 copy.220
  452.4 10.2 %all-reduce.36.cloned.1.call-done = f32[32,864]{1,0:T(8,128)} async-done(((f32[32,864]{1,0:T(8,128)}), f32[32,864]{1,0:T(8,128)}) %all-reduce.36.cloned.1.call-update) | async-done | bytes 110608 | tf_op jit(solution)/shard_map/psum | solution.py:201
  462.6 5.3 fusion.1
  467.9 127.7 %all-reduce.30 = (f32[]{:T(128)}, f32[32]{0:T(128)S(1)}, f32[32,64]{1,0:T(8,128)S(1)}, f32[64]{0:T(128)S(1)}, f32[64,2]{0,1:T(2,128)S(1)}) all-reduce(f32[]{:T(128)} %get-tuple-element.359, f32[32]{0:T(128)S(1)} %get-tuple-element.294, f32[32,64]{1,0:T(8,128)S(1)} %fusion.21, ...), channel_id=1, replica_groups=mesh['shell'=8,'sector'=32] {'sector'}, use_global_device_ids=true, to_apply=%region_10.11 | all-reduce | flops 2273 | bytes 18184 | tf_op jit(solution)/shard_map/psum | solution.py:170
  597.4 30.8 %all-reduce.31 = (f32[32]{0:T(128)}, f32[32,64]{1,0:T(8,128)}, f32[64]{0:T(128)}, f32[64,2]{0,1:T(2,128)}) all-reduce(f32[32]{0:T(128)S(1)} %get-tuple-element.283, f32[32,64]{1,0:T(8,128)S(1)} %get-tuple-element.284, f32[64]{0:T(128)S(1)} %get-tuple-element.285, ...), channel_id=1, replica_groups=mesh['shell'=8,'sector'=32] {'shell'}, use_global_device_ids=true, to_apply=%region_20.21 | all-reduce | flops 2272 | bytes 18176 | tf_op jit(solution)/shard_map/psum | solution.py:201
  (193 shorter events, 128.0 us)
Async XLA Ops:
  7.2 107.9 %copy-start = (bf16[32,864]{1,0:T(8,128)(2,1)S(1)}, bf16[32,864]{1,0:T(8,128)(2,1)}, u32[]{:S(2)}) copy-start(bf16[32,864]{1,0:T(8,128)(2,1)} %param.16) | copy-start | bytes 165892
  8.6 112.1 %all-to-all-start = ((s32[32,1,256]{2,1,0:T(1,128)}), s32[32,1,256]{2,1,0:T(1,128)S(1)}, u32[]{:S(2)}, u32[]{:S(2)}) async-start(s32[32,1,256]{2,1,0:T(1,128)} %all_to_all.12), calls=%async_computation | async-start | bytes 65536 | tf_op jit(solution)/shard_map/all_to_all | solution.py:119
  19.0 6.9 %copy-start.13 = (s32[1,4096]{1,0:T(1,128)S(1)}, s32[1,4096]{1,0:T(1,128)}, u32[]{:S(2)}) copy-start(s32[1,4096]{1,0:T(1,128)} %param.22) | copy-start | bytes 49156
  25.9 13.6 %copy-start.4 = (bf16[8,32,8,8,8]{1,4,3,2,0:T(8,128)(2,1)S(1)}, bf16[8,32,8,8,8]{1,4,3,2,0:T(8,128)(2,1)}, u32[]{:S(2)}) copy-start(bf16[8,32,8,8,8]{1,4,3,2,0:T(8,128)(2,1)} %get-tuple-element.350) | copy-start | bytes 786436
  40.6 22.6 %copy-start.3 = (bf16[8,32,8,8,8]{1,4,3,2,0:T(8,128)(2,1)S(1)}, bf16[8,32,8,8,8]{1,4,3,2,0:T(8,128)(2,1)}, u32[]{:S(2)}) copy-start(bf16[8,32,8,8,8]{1,4,3,2,0:T(8,128)(2,1)} %get-tuple-element.335) | copy-start | bytes 786436
  58.6 30.3 %copy-start.7 = (bf16[1,8,32,512]{3,2,1,0:T(8,128)(2,1)S(1)}, bf16[1,8,32,512]{3,2,1,0:T(8,128)(2,1)}, u32[]{:S(2)}) copy-start(bf16[1,8,32,512]{3,2,1,0:T(8,128)(2,1)} %param.15) | copy-start | bytes 786436
  64.2 32.3 %copy-start.2 = (bf16[8,32,8,8,8]{1,4,3,2,0:T(8,128)(2,1)S(1)}, bf16[8,32,8,8,8]{1,4,3,2,0:T(8,128)(2,1)}, u32[]{:S(2)}) copy-start(bf16[8,32,8,8,8]{1,4,3,2,0:T(8,128)(2,1)} %get-tuple-element.341) | copy-start | bytes 786436
  89.7 23.9 %copy-start.8 = (bf16[8,1,32,512]{3,2,1,0:T(8,128)(2,1)S(1)}, bf16[8,1,32,512]{3,2,1,0:T(8,128)(2,1)}, u32[]{:S(2)}) copy-start(bf16[8,1,32,512]{3,2,1,0:T(8,128)(2,1)} %copy.147) | copy-start | bytes 786436
  92.0 23.1 %copy-start.22 = (f32[32]{0:T(128)S(1)}, f32[32]{0:T(128)}, u32[]{:S(2)}) copy-start(f32[32]{0:T(128)} %param.17) | copy-start | bytes 388
  97.6 13.8 %copy-start.12 = (bf16[8,1,32,512]{3,2,1,0:T(8,128)(2,1)S(1)}, bf16[8,1,32,512]{3,2,1,0:T(8,128)(2,1)}, u32[]{:S(2)}) copy-start(bf16[8,1,32,512]{3,2,1,0:T(8,128)(2,1)} %copy.144) | copy-start | bytes 786436
  97.6 14.6 %copy-start.10 = (bf16[8,1,32,512]{3,2,1,0:T(8,128)(2,1)S(1)}, bf16[8,1,32,512]{3,2,1,0:T(8,128)(2,1)}, u32[]{:S(2)}) copy-start(bf16[8,1,32,512]{3,2,1,0:T(8,128)(2,1)} %copy.145) | copy-start | bytes 786436
  97.6 15.3 %copy-start.9 = (bf16[8,1,32,512]{3,2,1,0:T(8,128)(2,1)S(1)}, bf16[8,1,32,512]{3,2,1,0:T(8,128)(2,1)}, u32[]{:S(2)}) copy-start(bf16[8,1,32,512]{3,2,1,0:T(8,128)(2,1)} %copy.146) | copy-start | bytes 786436
  97.6 16.8 %copy-start.11 = (bf16[8,1,32,512]{3,2,1,0:T(8,128)(2,1)S(1)}, bf16[8,1,32,512]{3,2,1,0:T(8,128)(2,1)}, u32[]{:S(2)}) copy-start(bf16[8,1,32,512]{3,2,1,0:T(8,128)(2,1)} %copy.148) | copy-start | bytes 786436
  121.4 57.7 %copy-start.14 = (bf16[32,64]{1,0:T(8,128)(2,1)S(1)}, bf16[32,64]{1,0:T(8,128)(2,1)}, u32[]{:S(2)}) copy-start(bf16[32,64]{1,0:T(8,128)(2,1)} %param.18) | copy-start | bytes 12292
  121.4 57.7 %copy-start.23 = (f32[64]{0:T(128)S(1)}, f32[64]{0:T(128)}, u32[]{:S(2)}) copy-start(f32[64]{0:T(128)} %param.19) | copy-start | bytes 772
  145.5 34.5 %copy-start.24 = (f32[64,2]{0,1:T(2,128)S(1)}, f32[64,2]{0,1:T(2,128)}, u32[]{:S(2)}) copy-start(f32[64,2]{0,1:T(2,128)} %param.20) | copy-start | bytes 1540
  147.4 18.6 %all-to-all-start.1 = ((bf16[32,32,256]{2,0,1:T(8,128)(2,1)}), bf16[32,32,256]{2,0,1:T(8,128)(2,1)S(1)}, u32[]{:S(2)}, u32[]{:S(2)}) async-start(bf16[32,32,256]{2,0,1:T(8,128)(2,1)} %select_select_fusion), calls=%async_computation.1 | async-start | bytes 1048576 | tf_op jit(solution)/shard_map/all_to_all | solution.py:126
  154.8 54.2 %copy-start.21 = (f32[8]{0:T(128)}, f32[8]{0:T(128)S(1)}, u32[]{:S(2)}) copy-start(f32[8]{0:T(128)S(1)} %add_multiply_fusion.1) | copy-start | bytes 100
  154.8 70.2 %copy-start.16 = (s32[512]{0:T(512)S(1)}, s32[512]{0:T(512)}, u32[]{:S(2)}) copy-start(s32[512]{0:T(512)} %param.25) | copy-start | bytes 6148
  154.8 70.2 %copy-start.18 = (f32[512]{0:T(512)S(1)}, f32[512]{0:T(512)}, u32[]{:S(2)}) copy-start(f32[512]{0:T(512)} %param.24) | copy-start | bytes 6148
  154.8 70.2 %copy-start.19 = (f32[512]{0:T(512)S(1)}, f32[512]{0:T(512)}, u32[]{:S(2)}) copy-start(f32[512]{0:T(512)} %param.23) | copy-start | bytes 6148
  180.0 74.0 %copy-start.6 = (f32[64,4096]{1,0:T(8,128)}, f32[64,4096]{1,0:T(8,128)S(1)}, u32[]{:S(2)}) copy-start(f32[64,4096]{1,0:T(8,128)S(1)} %fusion) | copy-start | bytes 3145732
  225.0 1.2 copy-start.17
  225.1 1.2 copy-start.20
  226.3 0.9 copy-start.15
  274.7 21.1 %all-to-all-start.2 = ((f32[32,32,256]{2,0,1:T(8,128)}), f32[32,32,256]{2,0,1:T(8,128)S(1)}, u32[]{:S(2)}, u32[]{:S(2)}) async-start(f32[32,32,256]{2,0,1:T(8,128)} %copy.154), calls=%async_computation.2 | async-start | bytes 2097152 | tf_op jit(solution)/shard_map/all_to_all | solution.py:175
  279.0 183.6 %all-reduce.36.cloned.1.call-start = ((), (), s32[]{:S(2)}) async-start(), calls=%async_computation.3 | async-start | bytes 229376 | tf_op jit(solution)/shard_map/psum | solution.py:201
  283.0 61.0 %copy-start.5 = (f32[32,8,512]{2,0,1:T(8,128)S(1)}, f32[32,8,512]{2,0,1:T(8,128)}, u32[]{:S(2)}) copy-start(f32[32,8,512]{2,0,1:T(8,128)} %get-tuple-element.367) | copy-start | bytes 1572868
  357.8 270.3 %all-reduce.38.cloned.1.call-start = ((), (), s32[]{:S(2)}) async-start(), calls=%async_computation.4 | async-start | bytes 229376 | tf_op jit(solution)/shard_map/psum | solution.py:201
  462.6 167.1 %copy-start.1 = (bf16[32,864]{1,0:T(8,128)(2,1)S(1)}, bf16[32,864]{1,0:T(8,128)(2,1)}, u32[]{:S(2)}) copy-start(bf16[32,864]{1,0:T(8,128)(2,1)} %param.16) | copy-start | bytes 165892
Sparse Core Ops, SparseCore 0:
  357.9 104.6 all-reduce.35
  465.0 72.2 all-reduce.37
